TPU v7x, 768 devices: a whole 4x8x12 slice. The times are simulated.
768 devices in a mesh: pipe: 4 (over y_lo), fsdp: 96 (over x, z, y_hi), tp: 2 (over core).
Axes of the slice: x: 4, y: 8 (y_hi: 2, y_lo: 4; y = y_hi * 4 + y_lo), z: 12, core: 2. Of those that a mesh axis runs over, the one named last changes fastest.
Arguments:
- key_values: bfloat16 [4, 12288, 512], P('pipe', 'fsdp'), may hold values from -6 to 6
- projection: bfloat16 [4, 2, 32832, 128], P('pipe', 'tp', 'fsdp'), may hold values from -0.046875 to 0.046875
- queries: bfloat16 [4, 12288, 4096], P('pipe', 'fsdp'), may hold values from -240 to 240
- out_gradient: bfloat16 [4, 12288, 4096], P('pipe', 'fsdp'), may hold values from -6 to 6
- lengths: int32 [4, 96, 8], P('pipe', 'fsdp'), may hold values from 1 to 64, 128 in all within a row
- counts: int32 [4, 96], P('pipe', 'fsdp'), may hold values from 32 to 128, as said below
Outputs:
- upstream: bfloat16 [4, 12288, 16384], P('pipe', 'fsdp', 'tp')
Inputs may be any that keep to these rules, and one draw needn't show every extreme that they name: `counts`: in every phase some data rank has all 128 slots live.
All inputs are finite; a program needn't handle non-finite values.
Results may differ from a plain program's by a relative error of at most 0.0086.
Values may be sent and summed in bfloat16 or wider, within the bound.
A program may use at most 64 MiB of HBM per device.

v0:
```python
import jax
import jax.numpy as jnp
from jax import lax
from jax.sharding import Mesh
from jax.sharding import PartitionSpec as P

D = 16384
HD = 128
QH = 16
KVH = 2
FSDP = ("fsdp_0", "fsdp_1", "fsdp_2")


rotary_base = 500000.0


def joined_along(pieces, dim):
    pieces = jnp.moveaxis(pieces, 0, dim)
    shape = pieces.shape
    return pieces.reshape(*shape[:dim], shape[dim] * shape[dim + 1], *shape[dim + 2 :])


def stacked_from(value, axes, turns):
    pieces = value
    for k in turns:
        pieces = lax.all_gather(pieces, axes[k])
    done = turns[::-1]
    back = [done.index(k) for k in range(len(axes))]
    pieces = pieces.transpose(*back, *range(len(axes), pieces.ndim))
    return pieces.reshape(-1, *value.shape)


def whole_of(value, axes, turns, dim):
    return joined_along(stacked_from(value, axes, turns), dim)


def shifted(block, axis, distance):
    devices = range(lax.axis_size(axis))
    route = [(i - distance, i) for i in devices if i - distance in devices]
    return lax.ppermute(block, axis, route)


def rotary_tables(positions):
    half_width = HD // 2
    frequency = rotary_base ** (-(jnp.arange(half_width, dtype=jnp.float32) * 2.0 / HD))
    angle = positions.astype(jnp.float32)[:, None] * frequency[None, :]
    return (jnp.cos(angle), jnp.sin(angle))


def doc_layout(doc_lengths, live_count, row_count):
    row_index = jnp.arange(row_count, dtype=jnp.int32)
    doc_ends = jnp.cumsum(doc_lengths)
    segment = jnp.sum((row_index[:, None] >= doc_ends[None, :]).astype(jnp.int32), axis=1)
    doc_starts = doc_ends - doc_lengths
    doc_index = jnp.arange(doc_lengths.shape[0], dtype=jnp.int32)
    doc_first = jnp.sum(
        jnp.where(segment[:, None] == doc_index[None, :], doc_starts[None, :], 0), axis=1
    )
    positions = row_index - doc_first
    live_rows = row_index < live_count
    allowed = (segment[:, None] == segment[None, :]) & (row_index[None, :] <= row_index[:, None])
    allowed = allowed & live_rows[:, None] & live_rows[None, :]
    return (positions, allowed, live_rows)


def head_backward(queries, out_gradient, head_kv, cosine_table, sine_table, allowed, live_rows):
    row_count = queries.shape[0]
    score_scale = HD ** (-0.5)
    raw_keys = head_kv[:, :HD].astype(jnp.float32)
    first_half = raw_keys[:, : HD // 2]
    second_half = raw_keys[:, HD // 2 :]
    keys = jnp.concatenate(
        [
            first_half * cosine_table - second_half * sine_table,
            second_half * cosine_table + first_half * sine_table,
        ],
        axis=1,
    ).astype(jnp.bfloat16)
    values = head_kv[:, HD:]
    query_heads = queries.reshape(row_count, QH, HD)
    gradient_heads = out_gradient.reshape(row_count, QH, HD)
    scores = (
        jnp.einsum("thd,sd->hts", query_heads, keys, preferred_element_type=jnp.float32)
        * score_scale
    )
    masked = jnp.where(allowed[None], scores, -1e30)
    row_top = jnp.max(masked, axis=2, keepdims=True)
    exponent = jnp.where(allowed[None], jnp.exp(masked - row_top), 0.0)
    summed = jnp.sum(exponent, axis=2, keepdims=True)
    summed = jnp.where(live_rows[None, :, None], summed, 1.0)
    soft = exponent / summed
    soft_low = soft.astype(jnp.bfloat16)
    outputs = jnp.einsum("hts,sd->htd", soft_low, values, preferred_element_type=jnp.float32)
    row_delta = jnp.einsum("thd,htd->ht", gradient_heads.astype(jnp.float32), outputs)[:, :, None]
    prob_gradient = jnp.einsum(
        "thd,sd->hts", gradient_heads, values, preferred_element_type=jnp.float32
    )
    score_gradient = (soft * (prob_gradient - row_delta)).astype(jnp.bfloat16)
    key_gradient = (
        jnp.einsum("hts,thd->sd", score_gradient, query_heads, preferred_element_type=jnp.float32)
        * score_scale
    )
    value_gradient = jnp.einsum(
        "hts,thd->sd", soft_low, gradient_heads, preferred_element_type=jnp.float32
    )
    first_grad = key_gradient[:, : HD // 2]
    second_grad = key_gradient[:, HD // 2 :]
    return jnp.concatenate(
        [
            first_grad * cosine_table + second_grad * sine_table,
            second_grad * cosine_table - first_grad * sine_table,
            value_gradient,
        ],
        axis=1,
    ).astype(jnp.bfloat16)


def heads_backward(
    query_cols, grad_cols, kv_cols, head_total, cosine_table, sine_table, allowed, live_rows
):
    pieces = []
    for head in range(head_total):
        pieces.append(
            head_backward(
                query_cols[:, head * QH * HD : (head + 1) * QH * HD],
                grad_cols[:, head * QH * HD : (head + 1) * QH * HD],
                kv_cols[:, head * 2 * HD : (head + 1) * 2 * HD],
                cosine_table,
                sine_table,
                allowed,
                live_rows,
            )
        )
    return jnp.concatenate(pieces, axis=1)


def body(key_values, projection, queries, out_gradient, lengths, counts):
    own_strips = projection[0, 0]
    gathered = whole_of(own_strips, FSDP, (2, 0, 1), 0)
    tp_count = lax.axis_size("tp")
    half_width = D // tp_count
    columns = KVH * 2 * HD
    weight = gathered[: half_width * columns // 128].reshape(half_width, columns)
    saved = key_values[0]
    query_rows = queries[0]
    grad_rows = out_gradient[0]
    row_count = saved.shape[0]
    positions, allowed, live_rows = doc_layout(lengths[0, 0], counts[0, 0], row_count)
    cosine_table, sine_table = rotary_tables(positions)
    kv_gradient = heads_backward(
        query_rows, grad_rows, saved, KVH, cosine_table, sine_table, allowed, live_rows
    )
    input_gradient = lax.dot_general(
        kv_gradient, weight, (((1,), (1,)), ((), ())), preferred_element_type=jnp.float32
    )
    upstream = shifted(input_gradient.astype(jnp.bfloat16), "pipe", -1)
    return upstream[None]


def solution(mesh):
    split = Mesh(
        mesh.devices.reshape(mesh.shape["pipe"], 4, 12, 2, mesh.shape["tp"]),
        ("pipe", "fsdp_0", "fsdp_1", "fsdp_2", "tp"),
    )
    return jax.shard_map(
        body,
        mesh=split,
        in_specs=(
            P("pipe", FSDP, None),
            P("pipe", "tp", FSDP, None),
            P("pipe", FSDP, None),
            P("pipe", FSDP, None),
            P("pipe", FSDP, None),
            P("pipe", FSDP),
        ),
        out_specs=P("pipe", FSDP, "tp"),
        check_vma=False,
    )
```

profile of v0, /device:TPU:1, one launch (start us, length us, event | category | flops | bytes accessed | tf_op | source)
XLA Modules:
  0.0 254.2 jit_solution(99613903604071355)
XLA Ops:
  6.5 0.0 all-gather.5.cloned.1.call-start
  6.5 9.3 %all-gather = bf16[2,1,342,128]{3,2,1,0:T(8,128)(2,1)S(1)} all-gather(bf16[1,1,342,128]{3,2,1,0:T(8,128)(2,1)} %param.7), channel_id=2, replica_groups=mesh['pipe'=4,'fsdp_0'=4,'fsdp_1'=12,'fsdp_2'=2,'tp'=2] {'fsdp_2'}, dimensions={0}, use_global_device_ids=true | all-gather | bytes 262656 | tf_op jit(solution)/shard_map/all_gather | solution.py:26
  15.8 10.8 %all-gather.1 = bf16[8,1,342,128]{3,2,1,0:T(8,128)(2,1)S(1)} all-gather(bf16[2,1,342,128]{3,2,1,0:T(8,128)(2,1)S(1)} %all-gather), channel_id=3, replica_groups=mesh['pipe'=4,'fsdp_0'=4,'fsdp_1'=12,'fsdp_2'=2,'tp'=2] {'fsdp_0'}, dimensions={0}, use_global_device_ids=true | all-gather | bytes 875520 | tf_op jit(solution)/shard_map/all_gather | solution.py:26
  26.6 1.4 copy.118
  28.1 0.0 all-gather.5.cloned.1.call-update
  28.1 1.0 copy.99
  29.8 1.6 copy.100
  31.4 1.6 copy.103
  33.0 0.8 reduce-window.7
  33.9 0.1 convert_reduce_fusion
  33.9 0.7 bitcast_subtract_fusion
  34.6 0.1 select_reduce_fusion
  34.7 0.1 fusion.38
  34.8 0.2 fusion.64
  35.0 0.1 fusion.94
  35.1 0.0 copy-start
  35.1 0.0 copy-start.1
  35.1 1.5 fusion.95
  36.7 1.5 fusion.96
  38.2 0.0 copy-done
  38.2 1.8 fusion.34
  40.0 0.0 copy-done.1
  40.0 0.1 fusion.93
  40.1 0.3 fusion.18
  40.4 2.0 fusion.28
  42.3 0.2 fusion.76
  42.5 0.2 fusion.75
  42.8 0.3 fusion.31
  43.1 0.3 fusion.20
  43.4 2.0 fusion.29
  45.4 0.2 fusion.74
  45.6 0.2 fusion.73
  45.8 0.3 fusion.33
  46.1 98.5 %all-gather.5.cloned.1.call-done = bf16[48,2,342,128]{3,1,2,0:T(2,128)(2,1)} async-done(((bf16[4,2,342,128]{3,1,2,0:T(2,128)(2,1)}), bf16[48,2,342,128]{3,1,2,0:T(2,128)(2,1)}) %all-gather.5.cloned.1.call-update) | async-done | bytes 8405008 | tf_op jit(solution)/shard_map/all_gather | solution.py:26
  144.6 7.7 %copy.119 = bf16[48,2,342,128]{3,2,1,0:T(8,128)(2,1)} copy(bf16[48,2,342,128]{3,1,2,0:T(2,128)(2,1)} %all-gather.5.cloned.1.call-done) | data formatting | bytes 16809984 | tf_op jit(solution)/shard_map/all_gather | solution.py:26
  152.3 7.2 %copy.120 = bf16[4,12,2,342,128]{4,3,2,1,0:T(8,128)(2,1)} copy(bf16[4,12,2,342,128]{4,3,2,0,1:T(8,128)(2,1)} %bitcast.155) | data formatting | bytes 16809984 | tf_op jit(solution)/shard_map/transpose | solution.py:29
  159.6 11.1 %reshape_reshape.3 = bf16[32832,128]{1,0:T(8,128)(2,1)} reshape(bf16[4,12,2,342,128]{4,3,2,1,0:T(8,128)(2,1)} %copy.120) | data formatting | bytes 16809984 | tf_op jit(solution)/shard_map/reshape;reshape | solution.py:20
  170.6 7.0 %slice.90 = bf16[32768,128]{1,0:T(8,128)(2,1)} slice(bf16[32832,128]{1,0:T(8,128)(2,1)} %reshape_reshape.3), slice={[0:32768], [0:128]} | slice | bytes 16777216 | tf_op jit(solution)/shard_map/slice | solution.py:143
  177.7 13.9 %reshape.180 = bf16[8192,512]{1,0:T(8,128)(2,1)} reshape(bf16[32768,128]{1,0:T(8,128)(2,1)} %slice.90) | data formatting | bytes 16777216 | tf_op jit(solution)/shard_map/reshape | solution.py:143
  191.6 6.2 %convolution_convert_fusion = bf16[128,8192]{1,0:T(8,128)(2,1)S(1)} fusion(bf16[128,512]{0,1:T(8,128)(2,1)S(1)} %fusion.33, bf16[8192,512]{1,0:T(8,128)(2,1)} %reshape.180), kind=kOutput, calls=%fused_computation.2 | convolution fusion | flops 1074790400 | bytes 10616832 | tf_op jit(solution)/shard_map/dot_general | solution.py:153
  197.8 1.3 collective-permute-start
  199.1 46.9 %collective-permute-done = bf16[128,8192]{1,0:T(8,128)(2,1)S(1)} collective-permute-done((bf16[128,8192]{1,0:T(8,128)(2,1)S(1)}, bf16[128,8192]{1,0:T(8,128)(2,1)S(1)}, u32[]{:S(2)}, u32[]{:S(2)}) %collective-permute-start) | collective-permute-done | bytes 2097184 | tf_op jit(solution)/shard_map/ppermute | solution.py:40
  246.0 1.3 copy.160
  (5 shorter events, 0.0 us)
Async XLA Ops:
  6.5 138.1 %all-gather.5.cloned.1.call-start = ((), (), s32[]{:S(2)}) async-start(), calls=%async_computation | async-start | bytes 9105408 | tf_op jit(solution)/shard_map/all_gather | solution.py:26
  35.1 3.0 %copy-start = (bf16[128,2048]{0,1:T(8,128)(2,1)}, bf16[128,2048]{0,1:T(8,128)(2,1)S(1)}, u32[]{:S(2)}) copy-start(bf16[128,2048]{0,1:T(8,128)(2,1)S(1)} %get-tuple-element.7) | copy-start | bytes 1572868
  35.1 4.8 %copy-start.1 = (bf16[128,2048]{0,1:T(8,128)(2,1)}, bf16[128,2048]{0,1:T(8,128)(2,1)S(1)}, u32[]{:S(2)}) copy-start(bf16[128,2048]{0,1:T(8,128)(2,1)S(1)} %get-tuple-element.8) | copy-start | bytes 1572868
  197.8 48.2 %collective-permute-start = (bf16[128,8192]{1,0:T(8,128)(2,1)S(1)}, bf16[128,8192]{1,0:T(8,128)(2,1)S(1)}, u32[]{:S(2)}, u32[]{:S(2)}) collective-permute-start(bf16[128,8192]{1,0:T(8,128)(2,1)S(1)} %convolution_convert_fusion), channel_id=1, source_target_pairs={{192,0},{384,192},{576,384},{193,1},{385,193},{577,385},{194,2},{3... | collective-permute-start | bytes 6291464 | tf_op jit(solution)/shard_map/ppermute | solution.py:40
Sparse Core Ops, SparseCore 0:
  28.2 116.3 all-gather.4
where the time goes:
time: 255 us; the launch traced here: 254 us
  waiting for transfers between devices  145 us (57%)
  local copies, waits for them, and re-layouts  54.1 us (21%)
  blocking collectives  20.1 us (8%)
  matrix products  14.4 us (6%)
  between operations  14.2 us (6%)
  other arithmetic  4.67 us (2%)
    all_gather x1, waiting for transfers between devices, stacked_from(): pieces = lax.all_gather(pieces, axes[k])  98.5 us
    ppermute x1, waiting for transfers between devices, shifted(): return lax.ppermute(block, axis, route)  46.9 us
    all_gather x2, blocking collectives, stacked_from(): pieces = lax.all_gather(pieces, axes[k])  20.1 us
    reshape x1, local copies, waits for them, and re-layouts, body(): weight = gathered[:half_width * columns // 128].reshape(half_width, columns)  13.9 us
    another operation x1, local copies, waits for them, and re-layouts, joined_along(): pieces.reshape(*shape[:dim], shape[dim] * shape[dim + 1], *shape[dim + 2:])  11.1 us
    all_gather x2, local copies, waits for them, and re-layouts, stacked_from(): pieces = lax.all_gather(pieces, axes[k])  9.13 us
    transpose x1, local copies, waits for them, and re-layouts, stacked_from(): pieces = pieces.transpose(*back, *range(len(axes), pieces.ndim))  7.22 us
    slice x1, local copies, waits for them, and re-layouts, body(): weight = gathered[:half_width * columns // 128].reshape(half_width, columns)  7.05 us
  transfers between devices with their start and end apart: 2, of which 2 were waited for; matrix products, arithmetic and copies ran while one was open for 7% of the time, Pallas kernels for 0%

commit v1 on v0

v1 whole, which is shorter than its diff:
```python
import math

import jax
import jax.numpy as jnp
from jax import lax
from jax.experimental import pallas as pl
from jax.experimental.pallas import tpu as pltpu
from jax.sharding import Mesh
from jax.sharding import PartitionSpec as P

D = 16384
HD = 128
QH = 16
KVH = 2
TOK = 128
DOCS = 8
KV = KVH * 2 * HD
HEAD = QH * HD
NX, NZ, NYH, NYL = 4, 12, 2, 4
STRIPS = 342
ROWS = 88
PAIR = 171
LOCAL = PAIR * NZ
TILE = 128
TILES = 17
HALF = D // 2
ROTARY = 500000.0
READY = ((1, 0, 1), (2, 1, 3), (3, 3, 7), (4, 7, 9), (5, 9, 13), (6, 13, 17))
AXES = ("pipe", "fsdp_0", "fsdp_1", "fsdp_2", "tp")
MESH = pl.DeviceIdType.MESH
F32 = jnp.float32
BF16 = jnp.bfloat16
NT = (((1,), (1,)), ((), ()))


def dot(a, b, dims=(((1,), (0,)), ((), ()))):
    return lax.dot_general(a, b, dims, preferred_element_type=F32)


def iota(shape, dim):
    return lax.broadcasted_iota(jnp.int32, shape, dim)


def at(start, size):
    return pl.ds(pl.multiple_of(start, TILE), size)


def kernel(
    lengths,
    counts,
    kv_hbm,
    strips_hbm,
    q_hbm,
    g_hbm,
    out_hbm,
    kvin,
    strips,
    qbuf,
    gbuf,
    mine,
    piece,
    wp,
    xbuf,
    ybuf,
    rbuf,
    keys,
    masks,
    acc,
    load_sem,
    strip_send,
    strip_recv,
    ring_send,
    ring_recv,
    piece_sem,
    x_send,
    x_recv,
    pair_send,
    pair_recv,
    own_sem,
    y_send,
    y_recv,
    out_sem,
):
    p, x, z, h, c = [lax.axis_index(name) for name in AXES]
    rem, div = lax.rem, lax.div

    def load(src, dst, sem):
        copy = pltpu.make_async_copy(src, dst, load_sem.at[sem])
        copy.start()
        return copy

    strips_in = load(strips_hbm.at[0, 0], strips, 0)
    kv_in = load(kv_hbm.at[0, :, at(c * 2 * HD, 2 * HD)], kvin, 1)
    q_in = load(q_hbm.at[0, :, at(c * HEAD, HEAD)], qbuf, 2)
    g_in = load(g_hbm.at[0, :, at(c * HEAD, HEAD)], gbuf, 3)

    down_p = rem(p + NYL - 1, NYL)
    down_h = rem(h + 1 - div(p + NYL - 1, NYL), NYH)
    up_p = rem(p + 1, NYL)
    up_h = rem(h + div(p + 1, NYL), NYH)
    below = (down_p, x, z, down_h, c)
    far = (down_p, x, z, 1 - down_h, c)
    above = (up_p, x, z, up_h, c)
    far_up = (up_p, x, z, 1 - up_h, c)
    xs = [rem(x + k, NX) for k in range(NX)]
    x_at = [(p, xs[k], z, h, c) for k in range(NX)]
    z_up = (p, x, rem(z + 1, NZ), h, c)
    z_down = (p, x, rem(z + NZ - 1, NZ), h, c)
    partner = (p, x, z, h, 1 - c)

    barrier = pltpu.get_barrier_semaphore()
    friends = (below, far, above, far_up, x_at[1], x_at[2], x_at[3], z_up, z_down, partner)
    for friend in friends:
        pl.semaphore_signal(barrier, inc=1, device_id=friend, device_id_type=MESH)

    strips_in.wait()
    own = strips[...]
    for k in range(4):
        row, col = iota((ROWS, STRIPS), 0), iota((ROWS, STRIPS), 1)
        pick = (col == 4 * row + (k - 2 * h)).astype(F32).astype(BF16)
        mine[:, k * HD : (k + 1) * HD] = dot(pick, own).astype(BF16)

    pl.semaphore_wait(barrier, len(friends))

    sent = []

    def send(src, dst, send_sem, recv_sem, to):
        copy = pltpu.make_async_remote_copy(
            src_ref=src,
            dst_ref=dst,
            send_sem=send_sem,
            recv_sem=recv_sem,
            device_id=to,
            device_id_type=MESH,
        )
        copy.start()
        sent.append(copy)

    def arrived(ref, sem):
        pltpu.make_async_remote_copy(
            src_ref=ref,
            dst_ref=ref,
            send_sem=strip_send.at[0],
            recv_sem=sem,
            device_id=partner,
            device_id_type=MESH,
        ).wait_recv()

    for k, to in enumerate((below, far)):
        send(mine, wp.at[z, h], strip_send.at[k], strip_recv.at[k], to)

    row, col = iota((TOK, TOK), 0), iota((TOK, TOK), 1)
    end = jnp.int32(0)
    row_doc = jnp.zeros((TOK, TOK), jnp.int32)
    col_doc = jnp.zeros((TOK, TOK), jnp.int32)
    row_first = jnp.zeros((TOK, TOK), jnp.int32)
    for k in range(DOCS):
        length = lengths[0, 0, k]
        end = end + length
        past = row >= end
        row_doc = row_doc + past.astype(jnp.int32)
        row_first = row_first + jnp.where(past, length, 0)
        col_doc = col_doc + (col >= end).astype(jnp.int32)
    live = col < counts[0, 0]
    allowed = (row_doc == col_doc) & (row <= col) & live
    masks[0] = allowed.astype(F32)
    masks[1] = live.astype(F32)
    frequency = jnp.exp((col & (HD // 2 - 1)).astype(F32) * (-math.log(ROTARY) * 2.0 / HD))
    angle = (row - row_first).astype(F32) * frequency
    cosine = jnp.cos(angle)
    sine = jnp.sin(angle) * jnp.where(col < HD // 2, -1.0, 1.0)
    kv_in.wait()
    raw = kvin[:, :HD].astype(F32)
    keys[...] = (raw * cosine + pltpu.roll(raw, HD // 2, 1) * sine).astype(BF16)
    masks[2] = cosine
    masks[3] = sine
    acc[...] = jnp.zeros_like(acc)
    q_in.wait()
    g_in.wait()

    def one_head(head):
        scale = HD**-0.5
        q = qbuf[:, at(head * HD, HD)]
        g = gbuf[:, at(head * HD, HD)]
        scores = dot(keys[...], q, NT) * scale
        scores = jnp.where(masks[0] > 0.0, scores, -1e30)
        exponent = jnp.exp(scores - jnp.max(scores, axis=0, keepdims=True))
        summed = jnp.sum(exponent, axis=0, keepdims=True)
        soft = exponent * (masks[1, 0:1, :] / summed)
        low = soft.astype(BF16)
        prob = dot(kvin[:, HD:], g, NT)
        delta = jnp.sum(low.astype(F32) * prob, axis=0, keepdims=True)
        change = (soft * (prob - delta)).astype(BF16)
        return dot(change, q), dot(low, g)

    def some_heads(step, carry):
        parts = [one_head(4 * step + k) for k in range(4)]
        acc[:, :HD] += (parts[0][0] + parts[1][0]) + (parts[2][0] + parts[3][0])
        acc[:, HD:] += (parts[0][1] + parts[1][1]) + (parts[2][1] + parts[3][1])
        return carry

    lax.fori_loop(0, QH // 4, some_heads, 0)
    gradient = acc[:, :HD] * (HD**-0.5)
    turned = gradient * masks[2] - pltpu.roll(gradient, HD // 2, 1) * masks[3]
    wanted = p > 0
    piece[:, :HD] = jnp.where(wanted, turned, 0.0).astype(BF16)
    piece[:, HD:] = jnp.where(wanted, acc[:, HD:], 0.0).astype(BF16)
    cols = at(c * 2 * HD, 2 * HD)
    other_cols = at((1 - c) * 2 * HD, 2 * HD)
    send(piece, xbuf.at[x, :, cols], piece_sem.at[0], piece_sem.at[1], below)

    near_h = rem(h + div(p + 1, NYL), NYH)
    halves = (near_h, 1 - near_h)
    last = ((6, 5), (5, 6))

    def ring(kind, way, step):
        origin = rem(z + NZ - step, NZ) if way == 0 else rem(z + step, NZ)
        block = wp.at[origin, halves[kind]]
        if step == 0:
            if way == 0:
                arrived(block, strip_recv.at[kind])
        else:
            arrived(block, ring_recv.at[kind, way, step])
        if step < last[kind][way]:
            send(
                block,
                block,
                ring_send.at[kind, way, step + 1],
                ring_recv.at[kind, way, step + 1],
                (z_up, z_down)[way],
            )

    ring(0, 0, 0)
    ring(0, 1, 0)
    arrived(xbuf.at[x, :, cols], piece_sem.at[1])
    part = xbuf.at[x, :, cols]
    for k in (1, 3, 2):
        send(part, part, x_send.at[k], x_recv.at[NX - k], x_at[k])
    send(part, part, pair_send.at[0], pair_recv.at[0], partner)
    ring(1, 0, 0)
    ring(1, 1, 0)
    ring(0, 0, 1)
    ring(0, 1, 1)
    for k in (1, 3, 2):
        part = xbuf.at[xs[k], :, cols]
        arrived(part, x_recv.at[k])
        send(part, part, pair_send.at[k], pair_recv.at[k], partner)
    ring(1, 0, 1)
    ring(1, 1, 1)
    for k in range(NX):
        arrived(xbuf.at[xs[k], :, other_cols], pair_recv.at[k])

    def tile(k, carry):
        start = div(17 * z + 8, NZ)
        b = rem(start + 2 * TILES + div(k + 1, 2) * (2 * rem(k, 2) - 1), TILES)
        low = div(3 * b + 3, 4) - 1 + div(16 - b, 16)
        high = low + 1 - div(low + 1, NZ)
        r, i = iota((TILE, ROWS), 0), iota((TILE, ROWS), 1)
        feature = b * TILE - 4 * x + r
        inside = feature < LOCAL
        rows = None
        for m, source in enumerate((low, high)):
            for half in range(2):
                label = i + ((low + m) * PAIR + half * 85)
                pick = ((label == feature) & inside).astype(F32).astype(BF16)
                term = dot(pick, wp[source, half])
                rows = term if rows is None else rows + term
        weight = rows.astype(BF16)
        to = at((x * TILES + b) * TILE, TILE)
        for n in range(NX):
            result = dot(xbuf[xs[n]], weight, NT).astype(BF16)
            if n == 0:
                rbuf[:, to] = result
            else:
                ybuf[k, n - 1] = result
        for n in (2, 1, 3):
            pltpu.make_async_remote_copy(
                src_ref=ybuf.at[k, n - 1],
                dst_ref=rbuf.at[:, to],
                send_sem=y_send.at[n],
                recv_sem=y_recv.at[NX - n],
                device_id=x_at[n],
                device_id_type=MESH,
            ).start()
        return carry

    for step, first, stop in READY:
        if step > 1:
            ring(0, 0, step)
            if step <= last[0][1]:
                ring(0, 1, step)
            if step <= last[1][0]:
                ring(1, 0, step)
            ring(1, 1, step)
        lax.fori_loop(first, stop, tile, 0)

    span = TILES * TILE
    for n in range(1, NX):
        everything = rbuf.at[:, at(xs[n] * span, span)]
        arrived(everything, y_recv.at[n])
    for e in range(NX - 1):
        edge = rbuf[:, (17 * e + 16) * TILE : (17 * e + 17) * TILE]
        rbuf[:, 17 * (e + 1) * TILE : (17 * (e + 1) + 1) * TILE] += edge
    stores = []
    for n in range(NX):
        store = pltpu.make_async_copy(
            rbuf.at[:, n * span : n * span + 16 * TILE],
            out_hbm.at[0, :, n * 16 * TILE : (n + 1) * 16 * TILE],
            out_sem.at[n],
        )
        store.start()
        stores.append(store)
    for copy in sent:
        copy.wait_send()
    for n in range(1, NX):
        everything = rbuf.at[:, 0:span]
        pltpu.make_async_remote_copy(
            src_ref=everything,
            dst_ref=everything,
            send_sem=y_send.at[n],
            recv_sem=y_recv.at[n],
            device_id=x_at[n],
            device_id_type=MESH,
        ).wait_send()
    for store in stores:
        store.wait()


def body(key_values, projection, queries, out_gradient, lengths, counts):
    anywhere = pl.BlockSpec(memory_space=pl.ANY)
    scalars = pl.BlockSpec(memory_space=pltpu.SMEM)
    dma = pltpu.SemaphoreType.DMA
    return pl.pallas_call(
        kernel,
        out_shape=jax.ShapeDtypeStruct((1, TOK, HALF), BF16),
        in_specs=[scalars, scalars, anywhere, anywhere, anywhere, anywhere],
        out_specs=anywhere,
        scratch_shapes=[
            pltpu.VMEM((TOK, 2 * HD), BF16),
            pltpu.VMEM((STRIPS, HD), BF16),
            pltpu.VMEM((TOK, HEAD), BF16),
            pltpu.VMEM((TOK, HEAD), BF16),
            pltpu.VMEM((ROWS, KV), BF16),
            pltpu.VMEM((TOK, 2 * HD), BF16),
            pltpu.VMEM((NZ, NYH, ROWS, KV), BF16),
            pltpu.VMEM((NX, TOK, KV), BF16),
            pltpu.VMEM((TILES, NX - 1, TOK, TILE), BF16),
            pltpu.VMEM((TOK, NX * TILES * TILE), BF16),
            pltpu.VMEM((TOK, HD), BF16),
            pltpu.VMEM((4, TOK, TOK), F32),
            pltpu.VMEM((TOK, 2 * HD), F32),
            dma((4,)),
            dma((2,)),
            dma((2,)),
            dma((2, 2, 7)),
            dma((2, 2, 7)),
            dma((2,)),
            dma((NX,)),
            dma((NX,)),
            dma((NX,)),
            dma((NX,)),
            dma((1,)),
            dma((NX,)),
            dma((NX,)),
            dma((NX,)),
        ],
        compiler_params=pltpu.CompilerParams(collective_id=0, has_side_effects=True),
    )(lengths, counts, key_values, projection, queries, out_gradient)


def solution(mesh):
    split = Mesh(
        mesh.devices.reshape(mesh.shape["pipe"], NX, NZ, NYH, mesh.shape["tp"]),
        AXES,
    )
    fsdp = AXES[1:4]
    return jax.shard_map(
        body,
        mesh=split,
        in_specs=(
            P("pipe", fsdp, None),
            P("pipe", "tp", fsdp, None),
            P("pipe", fsdp, None),
            P("pipe", fsdp, None),
            P("pipe", fsdp, None),
            P("pipe", fsdp),
        ),
        out_specs=P("pipe", fsdp, "tp"),
        check_vma=False,
    )
```

time: 255 us -> 67 us (0.26)
  waiting for transfers between devices: 145 us -> 0 us
  Pallas kernels: 0 us -> 63 us
  local copies, waits for them, and re-layouts: 54.1 us -> 3.1 us
  blocking collectives: 20.1 us -> 0 us
  matrix products: 14.4 us -> 0 us
  between operations: 14.2 us -> 0.66 us
  other arithmetic: 4.67 us -> 0 us
    all_gather x1 -> x0, waiting for transfers between devices: 98.5 us -> none  [stacked_from(): pieces = lax.all_gather(pieces, axes[k])]
    pallas_call x0 -> x1, Pallas kernels: none -> 63 us  [body(): pl.pallas_call(kernel, out_shape=jax.ShapeDtypeStruct((1, TOK, HALF), BF1...]
    ppermute x1 -> x0, waiting for transfers between devices: 46.9 us -> none  [shifted(): return lax.ppermute(block, axis, route)]
    all_gather x2 -> x0, blocking collectives: 20.1 us -> none  [stacked_from(): pieces = lax.all_gather(pieces, axes[k])]
    reshape x1 -> x0, local copies, waits for them, and re-layouts: 13.9 us -> none  [body(): weight = gathered[:half_width * columns // 128].reshape(half_width, columns)]
    another operation x1 -> x0, local copies, waits for them, and re-layouts: 11.1 us -> none  [joined_along(): pieces.reshape(*shape[:dim], shape[dim] * shape[dim + 1], *shape[dim + 2:])]
    dot_general x5 -> x0, matrix products: 10.8 us -> none  [the longest x1 6.21 us: body(): lax.dot_general(kv_gradient, weight, (((1,), (1,)), ((), ())), preferred_...]
    all_gather x2 -> x0, local copies, waits for them, and re-layouts: 9.13 us -> none  [stacked_from(): pieces = lax.all_gather(pieces, axes[k])]
  transfers between devices with their start and end apart: 2 -> 0, of which waited for: 2 -> 0; matrix products, arithmetic and copies ran while one was open for 7% -> 0% of each run, Pallas kernels for 0% -> 0%
where the time goes in v1:
time: 67 us; the launch traced here: 66.8 us
  Pallas kernels  63 us (94%)
  local copies, waits for them, and re-layouts  3.1 us (5%)
    pallas_call x1, Pallas kernels, body(): pl.pallas_call(kernel, out_shape=jax.ShapeDtypeStruct((1, TOK, HALF), BF1...  63 us
    unnamed x1, local copies, waits for them, and re-layouts  3.1 us

profile of v1, /device:TPU:1, one launch (start us, length us, event | category | flops | bytes accessed | tf_op | source)
XLA Modules:
  0.0 66.8 jit_solution(4021941601227678217)
XLA Ops:
  0.7 63.0 %shard_map.64 = bf16[1,128,8192]{2,1,0:T(8,128)(2,1)} custom-call(s32[1,1,8]{2,1,0:T(1,128)} %lengths.1, s32[1,1]{1,0:T(1,128)S(6)} %copy.8.counts, bf16[1,128,512]{2,1,0:T(8,128)(2,1)} %kv_hbm.1, bf16[1,1,342,128]{3,2,1,0:T(8,128)(2,1)} %strips_hbm.1, bf16[1,128,4096]{2,1,0:T(8,128)(2,1)} %q_hbm.1, bf16[1,128,4096]{2,1,0:T(8,128)(2,1)} %g_hbm.1), custom_call_target="tpu_custom_call" | custom-call | tf_op jit(solution)/shard_map/pallas_call | solution.py:333
  63.7 3.1 %copy.9 = bf16[1,128,8192]{2,1,0:T(8,128)(2,1)} copy(bf16[1,128,8192]{2,1,0:T(8,128)(2,1)} %shard_map.64) | data formatting | bytes 4194304
